TPU v7x, 128 devices: a whole 4x4x4 slice. The times are simulated.
128 devices in a mesh: dom: 16 (over x, y), cls: 8 (over z, core).
Axes of the slice: x: 4, y: 4, z: 4, core: 2. Of those that a mesh axis runs over, the one named last changes fastest.
Arguments:
- stack: bfloat16 [32768, 2, 64, 128], P(('dom', 'cls')), may hold values from -6 to 6
- batch_index: int32 [16384], P(('dom', 'cls')), may hold values from 0 to 255, as said below
- best_class: int32 [16384], P(('dom', 'cls')), may hold values from 0 to 511, as said below
- best_rot: int32 [16384], P(('dom', 'cls')), may hold values from 0 to 63
- best_shift: int32 [16384, 2], P(('dom', 'cls')), may hold values from -4 to 4
- ctf: bfloat16 [16384, 64], P(('dom', 'cls')), may hold values from -1 to 1
- averages: float32 [512, 2, 64, 128], P(('dom', 'cls')), may hold values from -6 to 6
- velocity: float32 [512, 2, 64, 128], P(('dom', 'cls')), may hold values from -3 to 3
Outputs:
- new_averages: float32 [512, 2, 64, 128], P(('dom', 'cls'))
- new_velocity: float32 [512, 2, 64, 128], P(('dom', 'cls'))
- errors: float32 [16384], P(('dom', 'cls'))
Inputs may be any that keep to these rules, and one draw needn't show every extreme that they name: `batch_index`: each aligned block of 128 entries (one device's particles) holds distinct row numbers into that device's own 256 rows of stack. `best_class`: classes c with equal c // 32 form a group. In each aligned block of 128 entries (one device's particles) at most 16 entries name classes of one group, and some group is named by exactly 16 entries of that block.
All inputs are finite; a program needn't handle non-finite values.
Results may differ from a plain program's by a relative error of at most 0.0026.
Values may be sent and summed in bfloat16 or wider, within the bound.
No kernel may reach another device: no remote copies, remote signals or barrier semaphores. Data moves between devices by JAX's collectives and lax.ppermute only.
A program may use at most 128 MiB of HBM per device.

v0:
```python
import jax
import jax.numpy as jnp
from jax import lax
from jax.sharding import PartitionSpec as P

IMG = 128
TWO_PI = 6.283185307179586
MOMENTUM = 0.9
RATE = 0.5
RIDGE = 1.0


def align_rows(rows, rotation, shift):
    cycles = rows.shape[2]
    angles = rows.shape[3]
    radius = jnp.arange(cycles).astype(jnp.float32) + 1.0
    theta = TWO_PI * jnp.arange(angles).astype(jnp.float32) / angles
    shift_x = shift[:, 0].astype(jnp.float32)
    shift_y = shift[:, 1].astype(jnp.float32)
    along = (
        jnp.cos(theta)[None, None, :] * shift_x[:, None, None]
        + jnp.sin(theta)[None, None, :] * shift_y[:, None, None]
    )
    phase = TWO_PI * radius[None, :, None] * along / IMG
    cosine = jnp.cos(phase)
    sine = jnp.sin(phase)
    real = rows[:, 0].astype(jnp.float32)
    imag = rows[:, 1].astype(jnp.float32)
    turned = jnp.stack([cosine * real - sine * imag, sine * real + cosine * imag], axis=1).astype(
        jnp.bfloat16
    )
    source = (jnp.arange(angles)[None, :] + 2 * rotation[:, None]) % angles
    permute = (source[:, :, None] == jnp.arange(angles)[None, None, :]).astype(jnp.bfloat16)
    moved = jnp.einsum("pskb,pab->pska", turned, permute, preferred_element_type=jnp.float32)
    return moved.astype(jnp.bfloat16)


def class_table(marker, column):
    local = marker.astype(jnp.int32) - 1
    return (jnp.arange(column)[:, None] == local[None, :]).astype(jnp.bfloat16)


def class_partials(table, terms, gamma):
    grads = jnp.dot(table, terms, preferred_element_type=jnp.float32)
    gamma_float = gamma.astype(jnp.float32)
    weights = jnp.dot(
        table.astype(jnp.float32),
        gamma_float * gamma_float,
        precision=lax.Precision.HIGHEST,
        preferred_element_type=jnp.float32,
    )
    return (grads, weights)


def on_device(stack, batch_index, best_class, best_rot, best_shift, ctf, averages, velocity):
    count = batch_index.shape[0]
    cycles = ctf.shape[1]
    angles = stack.shape[3]
    stored = stack.shape[0]
    flat = 2 * cycles * angles
    owners = lax.axis_size("dom")
    column = lax.axis_size("cls") * averages.shape[0]
    slots = 2 * count // owners
    buffer_rows = owners * slots
    picker = (batch_index[:, None] == jnp.arange(stored)[None, :]).astype(jnp.bfloat16)
    rows = jnp.dot(picker, stack.reshape(stored, flat), preferred_element_type=jnp.float32)
    rows = rows.astype(jnp.bfloat16).reshape(count, 2, cycles, angles)
    aligned = align_rows(rows, best_rot, best_shift)
    owner = best_class // column
    local_class = best_class - owner * column
    placed = (owner[:, None] == jnp.arange(owners)[None, :]).astype(jnp.int32)
    position = jnp.sum(jnp.cumsum(placed, axis=0) * placed, axis=1) - 1
    target = owner * slots + position
    dispatch = (jnp.arange(buffer_rows)[:, None] == target[None, :]).astype(jnp.bfloat16)

    def pack(payload):
        packed = jnp.dot(dispatch, payload, preferred_element_type=jnp.float32).astype(jnp.bfloat16)
        return packed.reshape(owners, slots, payload.shape[1])

    ctf_packed = pack(ctf)
    marker_packed = pack((local_class + 1).astype(jnp.bfloat16)[:, None]).reshape(owners, slots)
    every = lax.all_gather(averages.astype(jnp.bfloat16), ("dom", "cls"), axis=0, tiled=True)
    total_classes = every.shape[0]
    chooser = (best_class[:, None] == jnp.arange(total_classes)[None, :]).astype(jnp.bfloat16)
    model = jnp.dot(
        chooser, every.reshape(total_classes, flat), preferred_element_type=jnp.float32
    ).reshape(count, 2, cycles, angles)
    gamma_wide = ctf.astype(jnp.float32)[:, None, :, None]
    resid = aligned.astype(jnp.float32) - gamma_wide * model
    errors = jnp.mean(resid * resid, axis=(1, 2, 3))
    term = (gamma_wide * resid).astype(jnp.bfloat16).reshape(count, flat)
    arrived = (
        lax.all_to_all(pack(term), "dom", split_axis=0, concat_axis=0, tiled=True),
        lax.all_to_all(ctf_packed, "dom", split_axis=0, concat_axis=0, tiled=True),
        lax.all_to_all(marker_packed, "dom", split_axis=0, concat_axis=0, tiled=True),
    )
    got_terms = arrived[0].reshape(buffer_rows, flat)
    got_gamma = arrived[1].reshape(buffer_rows, cycles)
    table = class_table(arrived[2].reshape(buffer_rows), column)
    grads, weights = class_partials(table, got_terms, got_gamma)
    summed, weight_sum = (
        lax.psum_scatter(grads, "cls", scatter_dimension=0, tiled=True),
        lax.psum_scatter(weights, "cls", scatter_dimension=0, tiled=True),
    )
    step = (summed.reshape(averages.shape) - RIDGE * averages) / (
        weight_sum[:, None, :, None] + RIDGE
    )
    new_velocity = MOMENTUM * velocity + step
    new_averages = averages + RATE * new_velocity
    return (new_averages, new_velocity, errors)


def solution(mesh):
    in_specs = (
        P(("dom", "cls"), None, None, None),
        P(("dom", "cls")),
        P(("dom", "cls")),
        P(("dom", "cls")),
        P(("dom", "cls"), None),
        P(("dom", "cls"), None),
        P(("dom", "cls"), None, None, None),
        P(("dom", "cls"), None, None, None),
    )
    out_specs = (
        P(("dom", "cls"), None, None, None),
        P(("dom", "cls"), None, None, None),
        P(("dom", "cls")),
    )
    return jax.shard_map(
        on_device, mesh=mesh, in_specs=in_specs, out_specs=out_specs, check_vma=False
    )
```

profile of v0, /device:TPU:0, one launch (start us, length us, event | category | flops | bytes accessed | tf_op | source)
XLA Modules:
  0.0 396.0 jit_solution(6878493428379385242)
XLA Ops:
  7.2 1.6 convert_element_type.118
  10.6 0.8 fusion.30
  11.4 0.7 all_to_all.16
  12.2 7.1 %all-to-all-start = ((bf16[16,1,16]{2,1,0:T(2,128)(2,1)}), bf16[16,1,16]{2,1,0:T(2,128)(2,1)S(1)}, u32[]{:S(2)}, u32[]{:S(2)}) async-start(bf16[16,1,16]{2,1,0:T(2,128)(2,1)} %all_to_all.16), calls=%async_computation | async-start | bytes 16384 | tf_op jit(solution)/shard_map/all_to_all | solution.py:95
  19.3 0.8 copy.19
  20.1 8.8 %fusion.24 = bf16[16,8,128,128]{3,1,2,0:T(8,128)(2,1)S(1)} fusion(bf16[32,8,128,128]{3,2,1,0:T(8,128)(2,1)} %bitcast.59, s32[128]{0:T(128)} %param.9), kind=kOutput, calls=%fused_computation.30 | convolution fusion | flops 1075871744 | bytes 12583424 | tf_op jit(solution)/shard_map/dot_general | solution.py:66
  28.9 1.2 copy.27
  30.5 17.4 %fusion.8 = (bf16[128,1,64,128]{3,2,1,0:T(8,128)(2,1)S(1)}, bf16[128,1,64,128]{3,2,1,0:T(8,128)(2,1)}) fusion(f32[128,128]{1,0:T(8,128)S(1)} %multiply_add_fusion.1, f32[64]{0:T(128)S(1)} %add_multiply_fusion, bf16[128,2,64,128]{3,2,1,0:T(8,128)(2,1)S(1)} %bitcast.58), kind=kLoop, calls=%fused_computation.17 | loop fusion | flops 12582912 | bytes 8454400 | tf_op jit(solution)/shard_map/convert
  47.9 46.7 %all-gather.2.cloned.1.call-done = bf16[512,2,64,128]{3,2,1,0:T(8,128)(2,1)} async-done(((bf16[4,2,64,128]{3,2,1,0:T(8,128)(2,1)}), bf16[512,2,64,128]{3,2,1,0:T(8,128)(2,1)}) %all-gather.2.cloned.1.call-update) | async-done | bytes 16777232 | tf_op jit(solution)/shard_map/all_gather | solution.py:82
  94.6 23.9 %copy.25 = bf16[512,2,64,128]{0,3,2,1:T(8,128)(2,1)} copy(bf16[512,2,64,128]{3,2,1,0:T(8,128)(2,1)} %all-gather.2.cloned.1.call-done) | data formatting | bytes 33554432 | tf_op jit(solution)/shard_map/reshape | solution.py:86
  118.5 13.6 %fusion = f32[128,2,64,128]{0,3,2,1:T(8,128)} fusion(bf16[512,2,64,128]{0,3,2,1:T(8,128)(2,1)} %copy.25, s32[128]{0:T(128)S(1)} %copy-done.4), kind=kOutput, calls=%fused_computation.2 | convolution fusion | flops 2147549184 | bytes 25166336 | tf_op jit(solution)/shard_map/dot_general | solution.py:85
  132.1 8.7 %copy.21 = f32[128,2,64,128]{3,2,1,0:T(8,128)} copy(f32[128,2,64,128]{0,3,2,1:T(8,128)} %fusion) | data formatting | bytes 16777216 | tf_op jit(solution)/shard_map/dot_general | solution.py:85
  140.8 9.4 %multiply_reduce_fusion = (f32[128]{0:T(128)S(1)}, bf16[128,2,64,128]{3,2,1,0:T(8,128)(2,1)S(1)}) fusion(f32[128,2,64,128]{3,2,1,0:T(8,128)} %copy.21, f32[128,64]{1,0:T(8,128)S(1)} %copy.19, s32[128,128]{1,0:T(8,128)S(1)} %add_select_fusion, bf16[128,1,64,128]{3,2,1,0:T(8,128)(2,1)} %get-tuple-element.8, bf16[128,1,64,128]{3,2,1,0:T(8,128)(2,1)S(1)} %get-tuple-element.7), kind=kOutput, calls=%fused_computation.6 | convolution fusion | flops 557842304 | bytes 16876032 | tf_op jit(solution)/shard_map/pskb,pab->pska/dot_general | solution.py:34
  150.2 6.7 %convolution_convert_fusion = bf16[256,16384]{1,0:T(8,128)(2,1)} fusion(bf16[16,8,128,128]{3,2,1,0:T(8,128)(2,1)S(1)} %bitcast.60, s32[128]{0:T(128)S(1)} %add_add_fusion), kind=kOutput, calls=%fused_computation | convolution fusion | flops 1077968896 | bytes 12583424 | tf_op jit(solution)/shard_map/dot_general | solution.py:77
  156.9 6.9 %all-to-all-start.1 = ((bf16[16,16,16384]{2,1,0:T(8,128)(2,1)}), bf16[16,16,16384]{2,1,0:T(8,128)(2,1)}, u32[]{:S(2)}, u32[]{:S(2)}) async-start(bf16[16,16,16384]{2,1,0:T(8,128)(2,1)} %bitcast.57), calls=%async_computation.1 | async-start | bytes 16777216 | tf_op jit(solution)/shard_map/all_to_all | solution.py:93
  163.9 146.1 %all-to-all-done.1 = bf16[16,16,16384]{2,1,0:T(8,128)(2,1)} async-done(((bf16[16,16,16384]{2,1,0:T(8,128)(2,1)}), bf16[16,16,16384]{2,1,0:T(8,128)(2,1)}, u32[]{:S(2)}, u32[]{:S(2)}) %all-to-all-start.1) | async-done | bytes 8388640 | tf_op jit(solution)/shard_map/all_to_all | solution.py:93
  310.0 6.3 %fusion.41 = f32[32,16384]{1,0:T(8,128)} fusion(bf16[256,16384]{1,0:T(8,128)(2,1)} %bitcast.12, s32[256]{0:T(256)S(1)} %sub.32), kind=kOutput, calls=%fused_computation.59 | convolution fusion | flops 268443648 | bytes 10486784 | tf_op jit(solution)/shard_map/dot_general | solution.py:44
  316.7 0.7 reshape.217
  317.4 11.7 %all-to-all-start.2 = ((bf16[16,2,512]{2,1,0:T(2,128)(2,1)}), bf16[16,2,512]{2,1,0:T(2,128)(2,1)S(1)}, u32[]{:S(2)}, u32[]{:S(2)}) async-start(bf16[16,2,512]{2,1,0:T(2,128)(2,1)} %reshape.217), calls=%async_computation.2 | async-start | bytes 65536 | tf_op jit(solution)/shard_map/all_to_all | solution.py:94
  330.3 6.4 %all-to-all-done.2 = bf16[16,2,512]{2,1,0:T(2,128)(2,1)S(1)} async-done(((bf16[16,2,512]{2,1,0:T(2,128)(2,1)}), bf16[16,2,512]{2,1,0:T(2,128)(2,1)S(1)}, u32[]{:S(2)}, u32[]{:S(2)}) %all-to-all-start.2) | async-done | bytes 32800 | tf_op jit(solution)/shard_map/all_to_all | solution.py:94
  337.0 23.6 %all-reduce.1 = f32[32,64]{1,0:T(8,128)S(1)} all-reduce(f32[32,64]{1,0:T(8,128)S(1)} %fusion.40), channel_id=3, replica_groups=mesh['dom'=16,'cls'=8] {'cls'}, use_global_device_ids=true, to_apply=%region_3.4.clone | all-reduce | flops 2048 | bytes 16384
  361.1 26.0 %all-reduce.4.cloned.1.call-done = f32[32,16384]{1,0:T(8,128)} async-done(((f32[32,16384]{1,0:T(8,128)}), f32[32,16384]{1,0:T(8,128)}) %all-reduce.4.cloned.1.call-update) | async-done | bytes 2097168
  387.0 1.1 dynamic-slice_bitcast_fusion
  388.2 1.0 multiply_add_fusion
  (42 shorter events, 4.0 us)
Async XLA Ops:
  7.2 87.4 %all-gather.2.cloned.1.call-start = ((), (), s32[]{:S(2)}) async-start(), calls=%async_computation.3 | async-start | bytes 16908288 | tf_op jit(solution)/shard_map/all_gather | solution.py:82
  12.2 144.8 %all-to-all-start = ((bf16[16,1,16]{2,1,0:T(2,128)(2,1)}), bf16[16,1,16]{2,1,0:T(2,128)(2,1)S(1)}, u32[]{:S(2)}, u32[]{:S(2)}) async-start(bf16[16,1,16]{2,1,0:T(2,128)(2,1)} %all_to_all.16), calls=%async_computation | async-start | bytes 16384 | tf_op jit(solution)/shard_map/all_to_all | solution.py:95
  28.9 1.3 copy-start.5
  28.9 1.3 copy-start.3
  47.9 70.6 %copy-start.4 = (s32[128]{0:T(128)S(1)}, s32[128]{0:T(128)}, u32[]{:S(2)}) copy-start(s32[128]{0:T(128)} %param.10) | copy-start | bytes 1540
  156.9 153.1 %all-to-all-start.1 = ((bf16[16,16,16384]{2,1,0:T(8,128)(2,1)}), bf16[16,16,16384]{2,1,0:T(8,128)(2,1)}, u32[]{:S(2)}, u32[]{:S(2)}) async-start(bf16[16,16,16384]{2,1,0:T(8,128)(2,1)} %bitcast.57), calls=%async_computation.1 | async-start | bytes 16777216 | tf_op jit(solution)/shard_map/all_to_all | solution.py:93
  163.8 223.3 %all-reduce.4.cloned.1.call-start = ((), (), s32[]{:S(2)}) async-start(), calls=%async_computation.4 | async-start | bytes 4194304
  310.0 6.3 %copy-start.2 = (bf16[128,64]{0,1:T(8,128)(2,1)S(1)}, bf16[128,64]{0,1:T(8,128)(2,1)}, u32[]{:S(2)}) copy-start(bf16[128,64]{0,1:T(8,128)(2,1)} %param.13) | copy-start | bytes 49156
  310.0 19.1 %copy-start.6 = (u32[128]{0:T(128)S(1)}, u32[128]{0:T(128)}, u32[]{:S(2)}) copy-start(u32[128]{0:T(128)} %constant.71) | copy-start | bytes 1540
  310.0 78.1 %copy-start = (f32[4,2,64,128]{3,2,1,0:T(8,128)S(1)}, f32[4,2,64,128]{3,2,1,0:T(8,128)}, u32[]{:S(2)}) copy-start(f32[4,2,64,128]{3,2,1,0:T(8,128)} %param.14) | copy-start | bytes 786436
  310.0 78.1 %copy-start.1 = (f32[4,2,64,128]{3,2,1,0:T(8,128)S(1)}, f32[4,2,64,128]{3,2,1,0:T(8,128)}, u32[]{:S(2)}) copy-start(f32[4,2,64,128]{3,2,1,0:T(8,128)} %param.15) | copy-start | bytes 786436
  317.4 19.3 %all-to-all-start.2 = ((bf16[16,2,512]{2,1,0:T(2,128)(2,1)}), bf16[16,2,512]{2,1,0:T(2,128)(2,1)S(1)}, u32[]{:S(2)}, u32[]{:S(2)}) async-start(bf16[16,2,512]{2,1,0:T(2,128)(2,1)} %reshape.217), calls=%async_computation.2 | async-start | bytes 65536 | tf_op jit(solution)/shard_map/all_to_all | solution.py:94
Sparse Core Ops, SparseCore 0:
  11.7 82.8 all-gather.1
  316.5 70.5 all-reduce.3
where the time goes:
time: 397 us; the launch traced here: 396 us
  waiting for transfers between devices  225 us (57%)
  matrix products  45.9 us (12%)
  local copies, waits for them, and re-layouts  38.1 us (10%)
  starting transfers between devices  25.8 us (6%)
  blocking collectives  23.6 us (6%)
  other arithmetic  22.6 us (6%)
  between operations  14.9 us (4%)
    all_to_all x1, waiting for transfers between devices, on_device(): lax.all_to_all(pack(term), 'dom', split_axis=0, concat_axis=0, tiled=True)  146 us
    all_gather x1, waiting for transfers between devices, on_device(): lax.all_gather(averages.astype(jnp.bfloat16), ('dom', 'cls'), axis=0, til...  46.7 us
    unnamed x3, waiting for transfers between devices  26 us
    reshape x1, local copies, waits for them, and re-layouts, on_device(): every.reshape(total_classes, flat)  23.9 us
    unnamed x1, blocking collectives  23.6 us
    another operation x1, other arithmetic  17.4 us
    dot_general x1, matrix products, on_device(): jnp.dot(chooser, every.reshape(total_classes, flat), preferred_element_ty...  13.6 us
    all_to_all x1, starting transfers between devices, on_device(): lax.all_to_all(ctf_packed, 'dom', split_axis=0, concat_axis=0, tiled=True)  11.7 us
  transfers between devices with their start and end apart: 5, of which 4 were waited for; matrix products, arithmetic and copies ran while one was open for 24% of the time, Pallas kernels for 0%

commit v1 on v0

--- a/solution.py
+++ b/solution.py
@@ -2,12 +2,19 @@
 import jax.numpy as jnp
 from jax import lax
 from jax.sharding import PartitionSpec as P
+from jax.lax import all_to_all, axis_size
 
 IMG = 128
 TWO_PI = 6.283185307179586
 MOMENTUM = 0.9
 RATE = 0.5
 RIDGE = 1.0
+feed_target = lambda arr_in: jnp.concatenate(
+    all_to_all(
+        jnp.stack(axis_size(("dom", "cls")) * [arr_in]), ("dom", "cls"), split_axis=0, concat_axis=0
+    ),
+    axis=0,
+)
 
 
 def align_rows(rows, rotation, shift):
@@ -79,7 +86,7 @@
 
     ctf_packed = pack(ctf)
     marker_packed = pack((local_class + 1).astype(jnp.bfloat16)[:, None]).reshape(owners, slots)
-    every = lax.all_gather(averages.astype(jnp.bfloat16), ("dom", "cls"), axis=0, tiled=True)
+    every = feed_target(averages.astype(jnp.bfloat16))
     total_classes = every.shape[0]
     chooser = (best_class[:, None] == jnp.arange(total_classes)[None, :]).astype(jnp.bfloat16)
     model = jnp.dot(

time: 397 us -> 590 us (1.49)
  waiting for transfers between devices: 225 us -> 367 us
  local copies, waits for them, and re-layouts: 38.1 us -> 67.5 us
  starting transfers between devices: 25.8 us -> 44.3 us
    all_to_all x0 -> x1, waiting for transfers between devices: none -> 200 us  [all_to_all(jnp.stack(axis_size(('dom', 'cls')) * [arr_in]), ('dom', 'cls'...]
    all_gather x1 -> x0, waiting for transfers between devices: 46.7 us -> none  [on_device(): lax.all_gather(averages.astype(jnp.bfloat16), ('dom', 'cls'), axis=0, til...]
    another operation x0 -> x2, local copies, waits for them, and re-layouts: none -> 31.6 us  [the longest x1 25.3 us: on_device(): every.reshape(total_classes, flat)]
    reshape x1 -> x0, local copies, waits for them, and re-layouts: 23.9 us -> none  [on_device(): every.reshape(total_classes, flat)]
    dot_general x1 -> x2, local copies, waits for them, and re-layouts: 8.66 us -> 31.1 us  [on_device(): jnp.dot(chooser, every.reshape(total_classes, flat), preferred_element_ty...]
    all_to_all x1, waiting for transfers between devices: 146 us -> 132 us  [on_device(): lax.all_to_all(pack(term), 'dom', split_axis=0, concat_axis=0, tiled=True)]
    all_to_all x0 -> x1, starting transfers between devices: none -> 11.7 us  [all_to_all(jnp.stack(axis_size(('dom', 'cls')) * [arr_in]), ('dom', 'cls'...]
    all_to_all x1, starting transfers between devices: 7.12 us -> 16.1 us  [on_device(): lax.all_to_all(marker_packed, 'dom', split_axis=0, concat_axis=0, tiled=T...]
  transfers between devices with their start and end apart: 5 -> 5, of which waited for: 4 -> 4; matrix products, arithmetic and copies ran while one was open for 24% -> 20% of each run, Pallas kernels for 0% -> 0%
where the time goes in v1:
time: 590 us; the launch traced here: 588 us
  waiting for transfers between devices  367 us (62%)
  local copies, waits for them, and re-layouts  67.5 us (11%)
  matrix products  45.3 us (8%)
  starting transfers between devices  44.3 us (8%)
  blocking collectives  28.4 us (5%)
  other arithmetic  20.6 us (3%)
  between operations  14.9 us (3%)
    all_to_all x1, waiting for transfers between devices, all_to_all(jnp.stack(axis_size(('dom', 'cls')) * [arr_in]), ('dom', 'cls'...  200 us
    all_to_all x1, waiting for transfers between devices, on_device(): lax.all_to_all(pack(term), 'dom', split_axis=0, concat_axis=0, tiled=True)  132 us
    dot_general x2, local copies, waits for them, and re-layouts, on_device(): jnp.dot(chooser, every.reshape(total_classes, flat), preferred_element_ty...  31.1 us
    unnamed x1, blocking collectives  28.4 us
    unnamed x2, waiting for transfers between devices  27.6 us
    another operation x1, local copies, waits for them, and re-layouts, on_device(): every.reshape(total_classes, flat)  25.3 us
    another operation x1, other arithmetic  17.4 us
    all_to_all x1, starting transfers between devices, on_device(): lax.all_to_all(marker_packed, 'dom', split_axis=0, concat_axis=0, tiled=T...  16.1 us
  transfers between devices with their start and end apart: 5, of which 4 were waited for; matrix products, arithmetic and copies ran while one was open for 20% of the time, Pallas kernels for 0%

profile of v1, /device:TPU:0, one launch (start us, length us, event | category | flops | bytes accessed | tf_op | source)
XLA Modules:
  0.0 587.8 jit_solution(2880282425286609938)
XLA Ops:
  7.2 1.0 convert_element_type.118
  8.1 6.3 %stack.6 = bf16[128,4,2,64,128]{4,3,2,1,0:T(8,128)(2,1)} broadcast(bf16[4,2,64,128]{3,2,1,0:T(8,128)(2,1)S(1)} %convert_element_type.118), dimensions={1,2,3,4} | broadcast | bytes 16908288 | tf_op jit(solution)/shard_map/stack | solution.py:14
  14.5 11.7 %all-to-all-start.1 = ((bf16[128,4,2,64,128]{4,3,2,1,0:T(8,128)(2,1)}), bf16[128,4,2,64,128]{4,3,2,1,0:T(8,128)(2,1)}, u32[]{:S(2)}, u32[]{:S(2)}) async-start(bf16[128,4,2,64,128]{4,3,2,1,0:T(8,128)(2,1)} %stack.6), calls=%async_computation.1 | async-start | bytes 33554432 | tf_op jit(solution)/shard_map/all_to_all | solution.py:13
  27.6 8.8 %fusion.22 = bf16[16,8,128,128]{3,1,2,0:T(8,128)(2,1)S(1)} fusion(bf16[32,8,128,128]{3,2,1,0:T(8,128)(2,1)} %bitcast.59, s32[128]{0:T(128)S(1)} %copy-done.4), kind=kOutput, calls=%fused_computation.28 | convolution fusion | flops 1075871744 | bytes 12583424 | tf_op jit(solution)/shard_map/dot_general | solution.py:73
  36.4 1.2 copy.26
  38.0 17.4 %fusion.6 = (bf16[128,1,64,128]{3,2,1,0:T(8,128)(2,1)S(1)}, bf16[128,1,64,128]{3,2,1,0:T(8,128)(2,1)}) fusion(f32[128,128]{1,0:T(8,128)S(1)} %multiply_add_fusion.1, f32[64]{0:T(128)S(1)} %add_multiply_fusion, bf16[128,2,64,128]{3,2,1,0:T(8,128)(2,1)S(1)} %bitcast.58), kind=kLoop, calls=%fused_computation.15 | loop fusion | flops 12582912 | bytes 8454400 | tf_op jit(solution)/shard_map/convert
  55.4 200.3 %all-to-all-done.1 = bf16[128,4,2,64,128]{4,3,2,1,0:T(8,128)(2,1)} async-done(((bf16[128,4,2,64,128]{4,3,2,1,0:T(8,128)(2,1)}), bf16[128,4,2,64,128]{4,3,2,1,0:T(8,128)(2,1)}, u32[]{:S(2)}, u32[]{:S(2)}) %all-to-all-start.1) | async-done | bytes 16777248 | tf_op jit(solution)/shard_map/all_to_all | solution.py:13
  255.7 16.1 %all-to-all-start = ((bf16[16,1,16]{2,1,0:T(2,128)(2,1)}), bf16[16,1,16]{2,1,0:T(2,128)(2,1)S(1)}, u32[]{:S(2)}, u32[]{:S(2)}) async-start(bf16[16,1,16]{2,1,0:T(2,128)(2,1)} %all_to_all.20), calls=%async_computation | async-start | bytes 16384 | tf_op jit(solution)/shard_map/all_to_all | solution.py:102
  271.8 25.3 %reshape_reshape.4 = bf16[512,16384]{1,0:T(8,128)(2,1)} reshape(bf16[128,4,2,64,128]{4,3,2,1,0:T(8,128)(2,1)} %all-to-all-done.1) | data formatting | bytes 33554432 | tf_op jit(solution)/shard_map/reshape;reshape | solution.py:93
  297.1 22.4 %copy.20 = bf16[16384,512]{1,0:T(8,128)(2,1)} copy(bf16[16384,512]{0,1:T(8,128)(2,1)} %bitcast.56) | data formatting | bytes 33554432 | tf_op jit(solution)/shard_map/dot_general | solution.py:92
  319.5 13.6 %fusion.26 = f32[128,2,64,128]{0,3,2,1:T(8,128)} fusion(bf16[2,64,128,512]{3,2,1,0:T(8,128)(2,1)} %bitcast.55, s32[128]{0:T(128)S(1)} %copy-done.5), kind=kOutput, calls=%fused_computation.35 | convolution fusion | flops 2147549184 | bytes 25166336 | tf_op jit(solution)/shard_map/dot_general | solution.py:92
  333.1 8.7 %copy.21 = f32[128,2,64,128]{3,2,1,0:T(8,128)} copy(f32[128,2,64,128]{0,3,2,1:T(8,128)} %fusion.26) | data formatting | bytes 16777216 | tf_op jit(solution)/shard_map/dot_general | solution.py:92
  341.8 9.4 %multiply_reduce_fusion = (f32[128]{0:T(128)S(1)}, bf16[128,2,64,128]{3,2,1,0:T(8,128)(2,1)S(1)}) fusion(f32[128,2,64,128]{3,2,1,0:T(8,128)} %copy.21, f32[128,64]{1,0:T(8,128)S(1)} %copy.19, s32[128,128]{1,0:T(8,128)S(1)} %add_select_fusion, bf16[128,1,64,128]{3,2,1,0:T(8,128)(2,1)} %get-tuple-element.8, bf16[128,1,64,128]{3,2,1,0:T(8,128)(2,1)S(1)} %get-tuple-element.7), kind=kOutput, calls=%fused_computation.4 | convolution fusion | flops 557842304 | bytes 16876032 | tf_op jit(solution)/shard_map/pskb,pab->pska/dot_general | solution.py:41
  351.3 6.7 %convolution_convert_fusion = bf16[256,16384]{1,0:T(8,128)(2,1)} fusion(bf16[16,8,128,128]{3,2,1,0:T(8,128)(2,1)S(1)} %bitcast.60, s32[128]{0:T(128)S(1)} %add_add_fusion), kind=kOutput, calls=%fused_computation | convolution fusion | flops 1077968896 | bytes 12583424 | tf_op jit(solution)/shard_map/dot_general | solution.py:84
  357.9 7.3 %all-to-all-start.2 = ((bf16[16,16,16384]{2,1,0:T(8,128)(2,1)}), bf16[16,16,16384]{2,1,0:T(8,128)(2,1)}, u32[]{:S(2)}, u32[]{:S(2)}) async-start(bf16[16,16,16384]{2,1,0:T(8,128)(2,1)} %bitcast.57), calls=%async_computation.2 | async-start | bytes 16777216 | tf_op jit(solution)/shard_map/all_to_all | solution.py:100
  365.4 132.5 %all-to-all-done.2 = bf16[16,16,16384]{2,1,0:T(8,128)(2,1)} async-done(((bf16[16,16,16384]{2,1,0:T(8,128)(2,1)}), bf16[16,16,16384]{2,1,0:T(8,128)(2,1)}, u32[]{:S(2)}, u32[]{:S(2)}) %all-to-all-start.2) | async-done | bytes 8388640 | tf_op jit(solution)/shard_map/all_to_all | solution.py:100
  497.9 6.3 %fusion.40 = f32[32,16384]{1,0:T(8,128)} fusion(bf16[256,16384]{1,0:T(8,128)(2,1)} %bitcast.11, s32[256]{0:T(256)S(1)} %sub.32), kind=kOutput, calls=%fused_computation.58 | convolution fusion | flops 268443648 | bytes 10486784 | tf_op jit(solution)/shard_map/dot_general | solution.py:51
  504.5 0.7 reshape.215
  505.2 9.2 %all-to-all-start.3 = ((bf16[16,2,512]{2,1,0:T(2,128)(2,1)}), bf16[16,2,512]{2,1,0:T(2,128)(2,1)S(1)}, u32[]{:S(2)}, u32[]{:S(2)}) async-start(bf16[16,2,512]{2,1,0:T(2,128)(2,1)} %reshape.215), calls=%async_computation.3 | async-start | bytes 65536 | tf_op jit(solution)/shard_map/all_to_all | solution.py:101
  515.7 6.4 %all-to-all-done.3 = bf16[16,2,512]{2,1,0:T(2,128)(2,1)S(1)} async-done(((bf16[16,2,512]{2,1,0:T(2,128)(2,1)}), bf16[16,2,512]{2,1,0:T(2,128)(2,1)S(1)}, u32[]{:S(2)}, u32[]{:S(2)}) %all-to-all-start.3) | async-done | bytes 32800 | tf_op jit(solution)/shard_map/all_to_all | solution.py:101
  522.3 28.4 %all-reduce.1 = f32[32,64]{1,0:T(8,128)S(1)} all-reduce(f32[32,64]{1,0:T(8,128)S(1)} %fusion.39), channel_id=3, replica_groups=mesh['dom'=16,'cls'=8] {'cls'}, use_global_device_ids=true, to_apply=%region_3.4.clone | all-reduce | flops 2048 | bytes 16384
  551.3 27.6 %all-reduce.4.cloned.1.call-done = f32[32,16384]{1,0:T(8,128)} async-done(((f32[32,16384]{1,0:T(8,128)}), f32[32,16384]{1,0:T(8,128)}) %all-reduce.4.cloned.1.call-update) | async-done | bytes 2097168
  578.9 1.1 dynamic-slice_bitcast_fusion
  580.0 1.0 multiply_add_fusion
  (45 shorter events, 3.5 us)
Async XLA Ops:
  14.4 11.7 %copy-start.5 = (s32[128]{0:T(128)S(1)}, s32[128]{0:T(128)}, u32[]{:S(2)}) copy-start(s32[128]{0:T(128)} %param.10) | copy-start | bytes 1540
  14.5 13.0 %copy-start.2 = (bf16[128,64]{0,1:T(8,128)(2,1)S(1)}, bf16[128,64]{0,1:T(8,128)(2,1)}, u32[]{:S(2)}) copy-start(bf16[128,64]{0,1:T(8,128)(2,1)} %param.13) | copy-start | bytes 49156
  14.5 13.1 %copy-start.4 = (s32[128]{0:T(128)S(1)}, s32[128]{0:T(128)}, u32[]{:S(2)}) copy-start(s32[128]{0:T(128)} %param.9) | copy-start | bytes 1540
  14.5 241.2 %all-to-all-start.1 = ((bf16[128,4,2,64,128]{4,3,2,1,0:T(8,128)(2,1)}), bf16[128,4,2,64,128]{4,3,2,1,0:T(8,128)(2,1)}, u32[]{:S(2)}, u32[]{:S(2)}) async-start(bf16[128,4,2,64,128]{4,3,2,1,0:T(8,128)(2,1)} %stack.6), calls=%async_computation.1 | async-start | bytes 33554432 | tf_op jit(solution)/shard_map/all_to_all | solution.py:13
  36.4 1.3 copy-start.6
  36.4 1.3 copy-start.3
  255.7 102.3 %all-to-all-start = ((bf16[16,1,16]{2,1,0:T(2,128)(2,1)}), bf16[16,1,16]{2,1,0:T(2,128)(2,1)S(1)}, u32[]{:S(2)}, u32[]{:S(2)}) async-start(bf16[16,1,16]{2,1,0:T(2,128)(2,1)} %all_to_all.20), calls=%async_computation | async-start | bytes 16384 | tf_op jit(solution)/shard_map/all_to_all | solution.py:102
  357.9 139.9 %all-to-all-start.2 = ((bf16[16,16,16384]{2,1,0:T(8,128)(2,1)}), bf16[16,16,16384]{2,1,0:T(8,128)(2,1)}, u32[]{:S(2)}, u32[]{:S(2)}) async-start(bf16[16,16,16384]{2,1,0:T(8,128)(2,1)} %bitcast.57), calls=%async_computation.2 | async-start | bytes 16777216 | tf_op jit(solution)/shard_map/all_to_all | solution.py:100
  365.2 213.6 %all-reduce.4.cloned.1.call-start = ((), (), s32[]{:S(2)}) async-start(), calls=%async_computation.4 | async-start | bytes 4194304
  497.9 16.5 %copy-start.7 = (u32[128]{0:T(128)S(1)}, u32[128]{0:T(128)}, u32[]{:S(2)}) copy-start(u32[128]{0:T(128)} %constant.71) | copy-start | bytes 1540
  497.9 82.1 %copy-start = (f32[4,2,64,128]{3,2,1,0:T(8,128)S(1)}, f32[4,2,64,128]{3,2,1,0:T(8,128)}, u32[]{:S(2)}) copy-start(f32[4,2,64,128]{3,2,1,0:T(8,128)} %param.14) | copy-start | bytes 786436
  497.9 82.1 %copy-start.1 = (f32[4,2,64,128]{3,2,1,0:T(8,128)S(1)}, f32[4,2,64,128]{3,2,1,0:T(8,128)}, u32[]{:S(2)}) copy-start(f32[4,2,64,128]{3,2,1,0:T(8,128)} %param.15) | copy-start | bytes 786436
  505.2 16.8 %all-to-all-start.3 = ((bf16[16,2,512]{2,1,0:T(2,128)(2,1)}), bf16[16,2,512]{2,1,0:T(2,128)(2,1)S(1)}, u32[]{:S(2)}, u32[]{:S(2)}) async-start(bf16[16,2,512]{2,1,0:T(2,128)(2,1)} %reshape.215), calls=%async_computation.3 | async-start | bytes 65536 | tf_op jit(solution)/shard_map/all_to_all | solution.py:101
Sparse Core Ops, SparseCore 0:
  504.3 74.4 all-reduce.3
